TPU v7x, 32 devices: a whole 2x2x4 slice. The times are simulated.
32 devices in a mesh: groups: 2 (over y), ep: 4 (over z), tp: 4 (over x, core).
Axes of the slice: x: 2, y: 2, z: 4, core: 2. Of those that a mesh axis runs over, the one named last changes fastest.
Arguments:
- tokens: bfloat16 [2, 512, 4096], P(None, ('groups', 'ep')), parts along dimension 1, may hold values from -6 to 6
- expert_ids: int32 [2, 512, 2], P(None, ('groups', 'ep')), parts along dimension 1, may hold values from 0 to 1, all different within a row
- gate_weights: float32 [2, 512, 2], P(None, ('groups', 'ep')), parts along dimension 1, may hold values from 0.05 to 1
- replica_pick: int32 [2, 512, 2], P(None, ('groups', 'ep')), parts along dimension 1, may hold values from 0 to 3
- placement: int32 [2, 4], replicated, may hold values from 0 to 1, as said below
- slot_limit: int32 [4], replicated, may hold values from 20 to 40, as said below
- expert_weights: bfloat16 [4, 3, 1536, 4096], P('ep', None, 'tp'), as said below
Outputs:
- layer_out: bfloat16 [2, 512, 4096], P(None, ('groups', 'ep'), 'tp'), parts along dimension 1
There are 2 independent parts, one for each index of `groups`. A program takes and returns all parts, laid end to end along the dimension named above; an argument that names none is the same for every part. Nothing has to cross between parts.
Inputs may be any that keep to these rules, and one draw needn't show every extreme that they name: `expert_ids`: each row names 2 different experts, and every expert is named somewhere. `placement`: row 0 is the old and row 1 the new slot-to-expert table. In each table every expert is held by one or more slots, and exactly 2 slots hold another expert in row 1 than in row 0. `slot_limit`: some slot has capacity exactly 40. `expert_weights`: slots that hold the same expert in the old table hold equal weights.
All inputs are finite; a program needn't handle non-finite values.
Results may differ from a plain program's by a relative error of at most 0.015.
Values may be sent and summed in bfloat16 or wider, within the bound.
A program may use at most 128 MiB of HBM per device.

v0:
```python
import functools

import jax
import jax.numpy as jnp
from jax import lax
from jax.experimental import pallas as pl
from jax.experimental.pallas import tpu as pltpu
from jax.sharding import PartitionSpec as P

MESH = pl.DeviceIdType.MESH


def kernel(
    E, T, tokens, ids, gates, replica, table, limits, placement, weights, out,
    w, x, p, r1, r2, y_send, y_recv, coef,
    w_sem, t_sem, zs, zr, xs, xr, cs, cr, as_, ar, bs, br, ys, yr,
):
    X = T // 2
    spans, top, rows = ids.shape
    slots = table.shape[1]
    s = lax.axis_index("ep")
    j = lax.axis_index("tp")
    side = lax.rem(j, 2)
    xi = j // 2
    partner = xi * 2 + (1 - side)
    width = x.shape[3]
    parts = [pl.ds(c * rows, rows) for c in range(spans)]

    reads = [
        pltpu.make_async_copy(tokens.at[:, pl.ds(q * width, width)], x.at[0, q], t_sem.at[q])
        for q in range(T)
    ]
    loads = [pltpu.make_async_copy(weights.at[0, i], w.at[i], w_sem.at[i]) for i in range(3)]
    for copy in reads:
        copy.start()
    for copy in loads:
        copy.start()

    barrier = pltpu.get_barrier_semaphore()
    for k in range(1, E):
        pl.semaphore_signal(barrier, inc=1, device_id={"ep": lax.rem(s + k, E)}, device_id_type=MESH)
    for m in range(1, X):
        pl.semaphore_signal(
            barrier, inc=1, device_id={"tp": lax.rem(xi + m, X) * 2 + side}, device_id_type=MESH
        )
    pl.semaphore_signal(barrier, inc=1, device_id={"tp": partner}, device_id_type=MESH)
    for copy in reads:
        copy.wait()
    pl.semaphore_wait(barrier, E - 1 + X)

    def remote(src, dst, send, recv, where):
        return pltpu.make_async_remote_copy(
            src_ref=src, dst_ref=dst, send_sem=send, recv_sem=recv, device_id=where, device_id_type=MESH
        )

    def peer(m):
        return lax.rem(xi + m, X) * 2 + side

    def source(m):
        return lax.rem(xi - m + X, X) * 2 + side

    def z_copy(k, c):
        return remote(
            x.at[0, j, parts[c]], x.at[k, j, parts[c]], zs.at[k, c], zr.at[k, c],
            {"ep": lax.rem(s - k + E, E)},
        )

    def x_copy(k, m, c):
        piece = x.at[k, j, parts[c]]
        return remote(piece, piece, xs.at[k, m, c], xr.at[k, m, c], {"tp": peer(m)})

    def x_arrival(k, m, c):
        piece = x.at[k, source(m), parts[c]]
        return remote(piece, piece, xs.at[k, m, c], xr.at[k, m, c], {"tp": peer(m)})

    def core_copy(k, m, c):
        piece = x.at[k, source(m), parts[c]]
        return remote(piece, piece, cs.at[k, m, c], cr.at[k, m, c], {"tp": partner})

    def core_arrival(k, m, c):
        piece = x.at[k, lax.rem(xi - m + X, X) * 2 + (1 - side), parts[c]]
        return remote(piece, piece, cs.at[k, m, c], cr.at[k, m, c], {"tp": partner})

    def half_copy(k):
        return remote(p.at[k, 1 - side], r1.at[k], as_.at[k], ar.at[k], {"tp": partner})

    def sum_copy(k, m, c):
        there = lax.rem(xi + m, X)
        return remote(
            p.at[k, side, there, parts[c]], r2.at[k, m, parts[c]], bs.at[k, m, c], br.at[k, m, c],
            {"tp": peer(m)},
        )

    def y_copy(k, c):
        return remote(
            y_send.at[k, parts[c]], y_recv.at[k, parts[c]], ys.at[k, c], yr.at[k, c],
            {"ep": lax.rem(s + k, E)},
        )

    for k in range(1, E):
        for c in range(spans):
            z_copy(k, c).start()

    lane = lax.broadcasted_iota(jnp.int32, (1, slots), 1)
    earlier_rows = (
        lax.broadcasted_iota(jnp.int32, (rows, rows), 0) > lax.broadcasted_iota(jnp.int32, (rows, rows), 1)
    ).astype(jnp.float32).astype(jnp.bfloat16)
    limit = limits[...].astype(jnp.float32)

    def holders(c):
        held = jnp.zeros((1, slots), jnp.int32)
        order = jnp.zeros((1, slots), jnp.int32)
        for other in range(slots):
            same = (table[c : c + 1, :] == placement[c, other]).astype(jnp.int32)
            held = held + same
            order = order + jnp.where(lane > other, same, 0)
        return held, order

    lowest = holders(0)[1] == 0
    for c in range(spans):
        held, order = holders(c)
        picks = []
        ids_c, gates_c, replica_c = ids[c].T, gates[c].T, replica[c].T
        for member in range(top):
            chosen = ids_c[:, member : member + 1]
            remaining = jnp.broadcast_to(replica_c[:, member : member + 1], (rows, slots))
            for _ in range(3):
                remaining = jnp.where(remaining >= held, remaining - held, remaining)
            hit = jnp.logical_and(chosen == table[c : c + 1, :], remaining == order)
            picks.append(hit.astype(jnp.float32))
        before = jnp.dot(
            earlier_rows, functools.reduce(jnp.add, picks).astype(jnp.bfloat16),
            preferred_element_type=jnp.float32,
        )
        scale = jnp.zeros((rows, slots), jnp.float32)
        for member in range(top):
            kept = jnp.sum(jnp.where(before < limit, picks[member], 0.0), axis=1, keepdims=True)
            before = before + picks[member]
            serves = jnp.logical_and(ids_c[:, member : member + 1] == table[0:1, :], lowest)
            scale = scale + jnp.where(serves, kept * gates_c[:, member : member + 1], 0.0)
        for slot in range(slots):
            coef[slot, c * rows : (c + 1) * rows, :] = scale[:, slot : slot + 1]

    for copy in loads:
        copy.wait()

    def compute(k):
        def project(i):
            total = None
            for q in range(T):
                part = lax.dot_general(
                    w[i, :, q * width : (q + 1) * width], x[k, q],
                    (((1,), (1,)), ((), ())), preferred_element_type=jnp.float32,
                )
                total = part if total is None else total + part
            return total

        gate = project(0)
        upward = project(1)
        hidden = (gate / (1.0 + jnp.exp(-gate)) * upward).T.astype(jnp.bfloat16)
        for q in range(T):
            p[k, q % 2, q // 2] = jnp.dot(
                hidden, w[2, :, q * width : (q + 1) * width], preferred_element_type=jnp.float32
            ).astype(jnp.bfloat16)

    def finish(k):
        for c in range(spans):
            total = p[k, side, xi, parts[c]].astype(jnp.float32)
            for m in range(1, X):
                sum_copy(k, m, c).wait_recv()
                total = total + r2[k, m, parts[c]].astype(jnp.float32)
            y_send[k, parts[c]] = total.astype(jnp.bfloat16)

            @pl.when(k >= 1)
            def _():
                y_copy(k, c).start()

    def step(k, carry):
        compute(k)
        half_copy(k).start()

        @pl.when(k + 1 < E)
        def _():
            for c in range(spans):
                z_copy(k + 1, c).wait_recv()
                for m in range(1, X):
                    x_copy(k + 1, m, c).start()
                core_copy(k + 1, 0, c).start()

        half_copy(k).wait_recv()
        for c in range(spans):
            for m in range(X):
                p[k, side, m, parts[c]] = (
                    p[k, side, m, parts[c]].astype(jnp.float32) + r1[k, m, parts[c]].astype(jnp.float32)
                ).astype(jnp.bfloat16)
            for m in range(1, X):
                sum_copy(k, m, c).start()

        @pl.when(k >= 1)
        def _():
            finish(k - 1)

        @pl.when(k + 1 < E)
        def _():
            for c in range(spans):
                for m in range(1, X):
                    x_arrival(k + 1, m, c).wait_recv()
                    core_copy(k + 1, m, c).start()
            for c in range(spans):
                for m in range(X):
                    core_arrival(k + 1, m, c).wait_recv()

        return carry

    lax.fori_loop(0, E, step, 0)
    finish(E - 1)

    def weigh(rows, scale):
        return jnp.where(scale != 0, rows.astype(jnp.float32) * scale, 0.0)

    def combine(k, total):
        for c in range(spans):
            y_copy(k, c).wait_recv()
        return total + weigh(y_recv[k], coef[lax.rem(s - k + E, E)])

    total = lax.fori_loop(1, E, combine, weigh(y_send[0], coef[s]))
    out[...] = total.astype(jnp.bfloat16)

    def drain(k, carry):
        half_copy(k).wait_send()
        for c in range(spans):
            for m in range(1, X):
                sum_copy(k, m, c).wait_send()

        @pl.when(k >= 1)
        def _():
            for c in range(spans):
                z_copy(k, c).wait_send()
                for m in range(1, X):
                    x_copy(k, m, c).wait_send()
                for m in range(X):
                    core_copy(k, m, c).wait_send()
                y_copy(k, c).wait_send()

        return carry

    lax.fori_loop(0, E, drain, 0)


def per_device(
    tokens, expert_ids, gate_weights, replica_pick, placement, slot_limit, expert_weights
):
    spans, rows, model_width = tokens.shape
    slots = placement.shape[1]
    E = lax.axis_size("ep")
    T = lax.axis_size("tp")
    X = T // 2
    width = model_width // T
    M = spans * rows
    hidden = expert_weights.shape[2]
    dma = pltpu.SemaphoreType.DMA
    out = pl.pallas_call(
        functools.partial(kernel, E, T),
        out_shape=jax.ShapeDtypeStruct((M, width), jnp.bfloat16),
        in_specs=[
            pl.BlockSpec(memory_space=pl.ANY),
            pl.BlockSpec(memory_space=pltpu.VMEM),
            pl.BlockSpec(memory_space=pltpu.VMEM),
            pl.BlockSpec(memory_space=pltpu.VMEM),
            pl.BlockSpec(memory_space=pltpu.VMEM),
            pl.BlockSpec(memory_space=pltpu.VMEM),
            pl.BlockSpec(memory_space=pltpu.SMEM),
            pl.BlockSpec(memory_space=pl.ANY),
        ],
        out_specs=pl.BlockSpec(memory_space=pltpu.VMEM),
        scratch_shapes=[
            pltpu.VMEM((3, hidden, model_width), jnp.bfloat16),
            pltpu.VMEM((E, T, M, width), jnp.bfloat16),
            pltpu.VMEM((E, 2, X, M, width), jnp.bfloat16),
            pltpu.VMEM((E, X, M, width), jnp.bfloat16),
            pltpu.VMEM((E, X, M, width), jnp.bfloat16),
            pltpu.VMEM((E, M, width), jnp.bfloat16),
            pltpu.VMEM((E, M, width), jnp.bfloat16),
            pltpu.VMEM((slots, M, 1), jnp.float32),
            dma((3,)), dma((T,)),
            dma((E, spans)), dma((E, spans)),
            dma((E, X, spans)), dma((E, X, spans)),
            dma((E, X, spans)), dma((E, X, spans)),
            dma((E,)), dma((E,)),
            dma((E, X, spans)), dma((E, X, spans)),
            dma((E, spans)), dma((E, spans)),
        ],
        compiler_params=pltpu.CompilerParams(
            collective_id=0, has_side_effects=True, vmem_limit_bytes=67043328
        ),
    )(
        tokens.reshape(M, model_width), jnp.swapaxes(expert_ids, 1, 2), jnp.swapaxes(gate_weights, 1, 2),
        jnp.swapaxes(replica_pick, 1, 2), placement,
        slot_limit.reshape(1, slots), placement, expert_weights,
    )
    return out.reshape(spans, rows, width)


def solution(mesh):
    placed = (
        P(None, ("groups", "ep"), None),
        P(None, ("groups", "ep"), None),
        P(None, ("groups", "ep"), None),
        P(None, ("groups", "ep"), None),
        P(),
        P(),
        P("ep", None, "tp", None),
    )
    return jax.shard_map(
        per_device,
        mesh=mesh,
        in_specs=placed,
        out_specs=P(None, ("groups", "ep"), "tp"),
        check_vma=False,
    )
```

profile of v0, /device:TPU:0, one launch (start us, length us, event | category | flops | bytes accessed | tf_op | source)
XLA Modules:
  0.0 69.0 jit_solution(7684184907339837638)
XLA Ops:
  0.0 67.4 %shard_map.73 = bf16[128,1024]{1,0:T(8,128)(2,1)} custom-call(bf16[128,4096]{1,0:T(8,128)(2,1)} %bitcast.6, s32[2,2,64]{2,1,0:T(2,128)} %bitcast.8, f32[2,2,64]{2,1,0:T(2,128)} %bitcast.9, s32[2,2,64]{2,1,0:T(2,128)} %bitcast.10, s32[2,4]{1,0:T(2,128)} %placement.1, s32[1,4]{1,0:T(1,128)} %bitcast.11, s32[2,4]{1,0:T(2,128)} %placement.1, ...), custom_call_target="tpu_custom_call" | custom-call | tf_op jit(solution)/shard_map/pallas_call | solution.py:262
  67.4 1.7 %copy.9 = bf16[2,64,1024]{2,1,0:T(8,128)(2,1)} copy(bf16[2,64,1024]{2,1,0:T(8,128)(2,1)} %bitcast.7) | data formatting | bytes 524288
where the time goes:
time: 69.4 us; the launch traced here: 69 us
  Pallas kernels  67.4 us (97%)
  local copies, waits for them, and re-layouts  1.67 us (2%)
    pallas_call x1, Pallas kernels, per_device(): pl.pallas_call(functools.partial(kernel, E, T), out_shape=jax.ShapeDtypeS...  67.4 us
    unnamed x1, local copies, waits for them, and re-layouts  1.67 us

commit v1 on v0

--- a/solution.py
+++ b/solution.py
@@ -247,6 +247,358 @@
     lax.fori_loop(0, E, drain, 0)
 
 
+def held_plan(pattern):
+    n = len(pattern)
+    groups = [[s for s in range(n) if pattern[s] == e] for e in (0, 1)]
+    host = [None] * n
+    load = [0] * n
+    order = sorted(range(n), key=lambda b: -len(groups[pattern[b]]))
+    for b in order:
+        others = groups[1 - pattern[b]]
+        best = min(others, key=lambda h: (load[h], abs(h - b), -abs(2 * h - n + 1)))
+        host[b] = best
+        load[best] += 1
+    served = [sorted((b for b in range(n) if host[b] == h), key=lambda b: abs(b - h)) for h in range(n)]
+    return host, served
+
+
+def routed_kernel(
+    E, host, served, phases, halves,
+    tokens, ids, gates, replica, table, limits, placement, weights, out,
+    w, x, p, r1, r2, y, y_recv,
+    w_sem, t_sem, zs, zr, xs, xr, cs, cr, as_, ar, bs, br, ys, yr,
+):
+    spans, top, rows = ids.shape
+    slots = table.shape[1]
+    M = spans * rows
+    unit = M // phases
+    s = lax.axis_index("ep")
+    j = lax.axis_index("tp")
+    side = lax.rem(j, 2)
+    xi = j // 2
+
+    def pick(values):
+        total = 0
+        for at, value in enumerate(values):
+            total = total + jnp.where(s == at, value, 0)
+        return total
+
+    depth = max(len(blocks) for blocks in served)
+    count = pick([len(blocks) for blocks in served])
+    target = pick(host)
+    place = pick([served[host[b]].index(b) for b in range(E)])
+
+    def block_of(i):
+        flat = 0
+        for at, blocks in enumerate(served):
+            for k, b in enumerate(blocks):
+                flat = flat + jnp.where(jnp.logical_and(s == at, i == k), b, 0)
+        return flat
+
+    reads = [pltpu.make_async_copy(tokens, x.at[0], t_sem.at[0])]
+    loads = [pltpu.make_async_copy(weights.at[0, i], w.at[i], w_sem.at[i]) for i in range(3)]
+    for copy in reads:
+        copy.start()
+    for copy in loads:
+        copy.start()
+
+    edges = sorted({tuple(sorted((b, host[b]))) for b in range(E)})
+    barrier = pltpu.get_barrier_semaphore()
+    for a, b in edges:
+        for me, other in ((a, b), (b, a)):
+            @pl.when(s == me)
+            def _():
+                pl.semaphore_signal(barrier, inc=1, device_id={"ep": other}, device_id_type=MESH)
+    core_peer = {"tp": xi * 2 + (1 - side)}
+    x_peer = {"tp": (1 - xi) * 2 + side}
+    pl.semaphore_signal(barrier, inc=1, device_id=core_peer, device_id_type=MESH)
+    pl.semaphore_signal(barrier, inc=1, device_id=x_peer, device_id_type=MESH)
+
+    def remote(src, dst, send, recv, where):
+        return pltpu.make_async_remote_copy(
+            src_ref=src, dst_ref=dst, send_sem=send, recv_sem=recv, device_id=where, device_id_type=MESH
+        )
+
+    quarter = unit // 4
+
+    def piece(item, u, xh, core, half):
+        if half:
+            return x.at[item, pl.ds(pl.multiple_of(u * unit + (2 * xh + core) * quarter, quarter), quarter)]
+        return x.at[item, pl.ds(pl.multiple_of(u * unit + core * 2 * quarter, 2 * quarter), 2 * quarter)]
+
+    def token_send(ph, half):
+        return remote(
+            piece(0, ph, xi, side, half), piece(ph + 1, place, xi, side, half), zs.at[ph], zr.at[ph, place],
+            {"ep": target},
+        )
+
+    def token_arrival(ph, i, half):
+        here = piece(ph + 1, i, xi, side, half)
+        return remote(here, here, zs.at[ph], zr.at[ph, i], {"ep": target})
+
+    def across(ph, i):
+        here = piece(ph + 1, i, xi, side, True)
+        return remote(here, here, xs.at[ph, i], xr.at[ph, i], x_peer)
+
+    def across_arrival(ph, i):
+        here = piece(ph + 1, i, 1 - xi, side, True)
+        return remote(here, here, xs.at[ph, i], xr.at[ph, i], x_peer)
+
+    def beside(ph, i, t, half):
+        here = piece(ph + 1, i, xi if t == 0 else 1 - xi, side, half)
+        return remote(here, here, cs.at[ph, i, t], cr.at[ph, i, t], core_peer)
+
+    def beside_arrival(ph, i, t, half):
+        here = piece(ph + 1, i, xi if t == 0 else 1 - xi, 1 - side, half)
+        return remote(here, here, cs.at[ph, i, t], cr.at[ph, i, t], core_peer)
+
+    def half_copy(item, u):
+        return remote(p.at[item, u, 1 - side], r1.at[item, u], as_.at[item, u], ar.at[item, u], core_peer)
+
+    def sum_copy(item, u):
+        return remote(p.at[item, u, side, 1 - xi], r2.at[item, u], bs.at[item, u], br.at[item, u], x_peer)
+
+    def y_copy(ph, i):
+        return remote(y.at[ph + 1, i], y_recv.at[ph], ys.at[ph, i], yr.at[ph], {"ep": block_of(i)})
+
+    def y_arrival(ph):
+        return remote(y.at[ph + 1, 0], y_recv.at[ph], ys.at[ph, 0], yr.at[ph], {"ep": target})
+
+    def both(ph, action):
+        if halves <= 0:
+            action(False)
+        elif halves >= phases:
+            action(True)
+        else:
+            pl.when(ph < halves)(lambda: action(True))
+            pl.when(ph >= halves)(lambda: action(False))
+
+    lane = lax.broadcasted_iota(jnp.int32, (1, slots), 1)
+    earlier_rows = (
+        lax.broadcasted_iota(jnp.int32, (rows, rows), 0) > lax.broadcasted_iota(jnp.int32, (rows, rows), 1)
+    ).astype(jnp.float32).astype(jnp.bfloat16)
+    limit = limits[...].astype(jnp.float32)
+    own_expert = placement[0, s]
+
+    def holders(c):
+        held = jnp.zeros((1, slots), jnp.int32)
+        order = jnp.zeros((1, slots), jnp.int32)
+        for other in range(slots):
+            same = (table[c : c + 1, :] == placement[c, other]).astype(jnp.int32)
+            held = held + same
+            order = order + jnp.where(lane > other, same, 0)
+        return held, order
+
+    scales = []
+    for c in range(spans):
+        held, order = holders(c)
+        picks = []
+        ids_c, gates_c, replica_c = ids[c].T, gates[c].T, replica[c].T
+        for member in range(top):
+            chosen = ids_c[:, member : member + 1]
+            remaining = jnp.broadcast_to(replica_c[:, member : member + 1], (rows, slots))
+            for _ in range(3):
+                remaining = jnp.where(remaining >= held, remaining - held, remaining)
+            hit = jnp.logical_and(chosen == table[c : c + 1, :], remaining == order)
+            picks.append(hit.astype(jnp.float32))
+        before = jnp.dot(
+            earlier_rows, functools.reduce(jnp.add, picks).astype(jnp.bfloat16),
+            preferred_element_type=jnp.float32,
+        )
+        here = jnp.zeros((rows, 1), jnp.float32)
+        there = jnp.zeros((rows, 1), jnp.float32)
+        for member in range(top):
+            kept = jnp.sum(jnp.where(before < limit, picks[member], 0.0), axis=1, keepdims=True)
+            before = before + picks[member]
+            scaled = kept * gates_c[:, member : member + 1]
+            own = ids_c[:, member : member + 1] == own_expert
+            here = here + jnp.where(own, scaled, 0.0)
+            there = there + jnp.where(own, 0.0, scaled)
+        scales.append((here, there))
+
+    for copy in reads:
+        copy.wait()
+    pl.semaphore_wait(barrier, 2 + pick([sum(1 for e in edges if v in e) for v in range(E)]))
+
+    for ph in range(phases):
+        token_send(ph, ph < halves).start()
+
+    for copy in loads:
+        copy.wait()
+
+    def units(item):
+        return jnp.where(item == 0, phases, count)
+
+    def gather(ph):
+        def first(i, carry):
+            def go(half):
+                token_arrival(ph, i, half).wait_recv()
+                if half:
+                    across(ph, i).start()
+                beside(ph, i, 0, half).start()
+            both(ph, go)
+            return carry
+
+        def second(i, carry):
+            def go(half):
+                if half:
+                    across_arrival(ph, i).wait_recv()
+                    beside(ph, i, 1, half).start()
+            both(ph, go)
+            return carry
+
+        def third(i, carry):
+            def go(half):
+                beside_arrival(ph, i, 0, half).wait_recv()
+                if half:
+                    beside_arrival(ph, i, 1, half).wait_recv()
+            both(ph, go)
+            return carry
+
+        lax.fori_loop(0, count, first, 0)
+        if halves > 0:
+            lax.fori_loop(0, count, second, 0)
+        lax.fori_loop(0, count, third, 0)
+
+    width = y.shape[3]
+    T = 4
+
+    def compute(item):
+        def project(i):
+            return lax.dot_general(
+                w[i], x[item], (((1,), (1,)), ((), ())), preferred_element_type=jnp.float32
+            )
+
+        gate = project(0)
+        upward = project(1)
+        hidden = (gate / (1.0 + jnp.exp(-gate)) * upward).T.astype(jnp.bfloat16)
+        for q in range(T):
+            part = jnp.dot(
+                hidden, w[2, :, q * width : (q + 1) * width], preferred_element_type=jnp.float32
+            ).astype(jnp.bfloat16)
+            for u in range(phases):
+                p[item, u, q % 2, q // 2] = part[u * unit : (u + 1) * unit]
+
+    def reduce(item):
+        def one(u, carry):
+            half_copy(item, u).wait_recv()
+            for m in range(2):
+                p[item, u, side, m] = (
+                    p[item, u, side, m].astype(jnp.float32) + r1[item, u, m].astype(jnp.float32)
+                ).astype(jnp.bfloat16)
+            sum_copy(item, u).start()
+            return carry
+
+        lax.fori_loop(0, units(item), one, 0)
+
+    def finish(item):
+        def one(u, carry):
+            sum_copy(item, u).wait_recv()
+            y[item, u] = (
+                p[item, u, side, xi].astype(jnp.float32) + r2[item, u].astype(jnp.float32)
+            ).astype(jnp.bfloat16)
+
+            @pl.when(item >= 1)
+            def _():
+                y_copy(item - 1, u).start()
+
+            return carry
+
+        lax.fori_loop(0, units(item), one, 0)
+
+    items = jnp.where(count > 0, phases + 1, 1)
+
+    def step(item, carry):
+        pl.when(item >= 1)(lambda: gather(item - 1))
+        compute(item)
+
+        def send(u, carry):
+            half_copy(item, u).start()
+            return carry
+
+        lax.fori_loop(0, units(item), send, 0)
+        pl.when(item >= 1)(lambda: finish(item - 1))
+        reduce(item)
+        return carry
+
+    lax.fori_loop(0, items, step, 0)
+    finish(items - 1)
+
+    def weigh(values, scale):
+        return jnp.where(scale != 0, values.astype(jnp.float32) * scale, 0.0)
+
+    here = jnp.concatenate([scale[0] for scale in scales], axis=0)
+    there = jnp.concatenate([scale[1] for scale in scales], axis=0)
+    for ph in range(phases):
+        y_arrival(ph).wait_recv()
+        at = slice(ph * unit, (ph + 1) * unit)
+        out[at] = (weigh(y[0, ph], here[at]) + weigh(y_recv[ph], there[at])).astype(jnp.bfloat16)
+
+    for ph in range(phases):
+        token_send(ph, ph < halves).wait_send()
+
+    def drain(item, carry):
+        def one(u, carry):
+            half_copy(item, u).wait_send()
+            sum_copy(item, u).wait_send()
+
+            @pl.when(item >= 1)
+            def _():
+                ph = item - 1
+                y_copy(ph, u).wait_send()
+
+                def go(half):
+                    beside(ph, u, 0, half).wait_send()
+                    if half:
+                        across(ph, u).wait_send()
+                        beside(ph, u, 1, half).wait_send()
+                both(ph, go)
+
+            return carry
+
+        return lax.fori_loop(0, units(item), one, carry)
+
+    lax.fori_loop(0, items, drain, 0)
+
+
+def routed(code, pattern, args, spans, rows, slots, E, hidden, model_width, width):
+    host, served = held_plan(pattern)
+    depth = max(len(blocks) for blocks in served)
+    phases = 4 if depth > 1 else 2
+    lone = [h for h in range(E) if len(served[h]) == depth]
+    halves = 2 if depth > 1 and lone[0] in (0, E - 1) else 0
+    halves = min(halves, phases)
+    M = spans * rows
+    unit = M // phases
+    dma = pltpu.SemaphoreType.DMA
+    any_, vmem, smem = (pl.BlockSpec(memory_space=space) for space in (pl.ANY, pltpu.VMEM, pltpu.SMEM))
+    return pl.pallas_call(
+        functools.partial(routed_kernel, E, host, served, phases, halves),
+        out_shape=jax.ShapeDtypeStruct((M, width), jnp.bfloat16),
+        in_specs=[any_, vmem, vmem, vmem, vmem, vmem, smem, any_],
+        out_specs=vmem,
+        scratch_shapes=[
+            pltpu.VMEM((3, hidden, model_width), jnp.bfloat16),
+            pltpu.VMEM((phases + 1, M, model_width), jnp.bfloat16),
+            pltpu.VMEM((phases + 1, phases, 2, 2, unit, width), jnp.bfloat16),
+            pltpu.VMEM((phases + 1, phases, 2, unit, width), jnp.bfloat16),
+            pltpu.VMEM((phases + 1, phases, unit, width), jnp.bfloat16),
+            pltpu.VMEM((phases + 1, phases, unit, width), jnp.bfloat16),
+            pltpu.VMEM((phases, unit, width), jnp.bfloat16),
+            dma((3,)), dma((1,)),
+            dma((phases,)), dma((phases, depth)),
+            dma((phases, depth)), dma((phases, depth)),
+            dma((phases, depth, 2)), dma((phases, depth, 2)),
+            dma((phases + 1, phases)), dma((phases + 1, phases)),
+            dma((phases + 1, phases)), dma((phases + 1, phases)),
+            dma((phases, depth)), dma((phases,)),
+        ],
+        compiler_params=pltpu.CompilerParams(
+            collective_id=code, has_side_effects=True, vmem_limit_bytes=67043328
+        ),
+    )(*args)
+
+
 def per_device(
     tokens, expert_ids, gate_weights, replica_pick, placement, slot_limit, expert_weights
 ):
@@ -259,6 +611,30 @@
     M = spans * rows
     hidden = expert_weights.shape[2]
     dma = pltpu.SemaphoreType.DMA
+    args = (
+        tokens.reshape(M, model_width), jnp.swapaxes(expert_ids, 1, 2), jnp.swapaxes(gate_weights, 1, 2),
+        jnp.swapaxes(replica_pick, 1, 2), placement,
+        slot_limit.reshape(1, slots), placement, expert_weights,
+    )
+    if expert_ids.shape[2] == 2 and slots == 4 and E == slots and X == 2:
+        patterns = [tuple((0,) + tuple((m >> b) & 1 for b in range(slots - 1))) for m in range(1, 2 ** (slots - 1))]
+        old = placement[0]
+        weight = jnp.array([0] + [1 << b for b in range(slots - 1)], jnp.int32)
+        which = jnp.sum(jnp.where(old != old[0], weight, 0)) - 1
+        out = lax.switch(
+            which,
+            [
+                functools.partial(
+                    lambda code, pattern, *args: routed(
+                        code, pattern, args, spans, rows, slots, E, hidden, model_width, width
+                    ),
+                    code, pattern,
+                )
+                for code, pattern in enumerate(patterns)
+            ],
+            *args,
+        )
+        return out.reshape(spans, rows, width)
     out = pl.pallas_call(
         functools.partial(kernel, E, T),
         out_shape=jax.ShapeDtypeStruct((M, width), jnp.bfloat16),
@@ -293,11 +669,7 @@
         compiler_params=pltpu.CompilerParams(
             collective_id=0, has_side_effects=True, vmem_limit_bytes=67043328
         ),
-    )(
-        tokens.reshape(M, model_width), jnp.swapaxes(expert_ids, 1, 2), jnp.swapaxes(gate_weights, 1, 2),
-        jnp.swapaxes(replica_pick, 1, 2), placement,
-        slot_limit.reshape(1, slots), placement, expert_weights,
-    )
+    )(*args)
     return out.reshape(spans, rows, width)
 
 

time: 69.4 us -> 61.3 us (0.88)
  Pallas kernels: 67.4 us -> 54.8 us
  other arithmetic: 0 us -> 1.97 us
  local copies, waits for them, and re-layouts: 1.67 us -> 2.86 us
    pallas_call x1, Pallas kernels: 67.4 us -> 54.8 us  [routed(): pl.pallas_call(functools.partial(routed_kernel, E, host, served, phases,...]
    reduce_sum x0 -> x1, other arithmetic: none -> 1.97 us  [per_device(): which = jnp.sum(jnp.where(old != old[0], weight, 0)) - 1]
    slice x0 -> x1, local copies, waits for them, and re-layouts: none -> 1.19 us  [per_device(): which = jnp.sum(jnp.where(old != old[0], weight, 0)) - 1]
where the time goes in v1:
time: 61.3 us; the launch traced here: 60.5 us
  Pallas kernels  54.8 us (89%)
  local copies, waits for them, and re-layouts  2.86 us (5%)
  other arithmetic  1.97 us (3%)
    pallas_call x1, Pallas kernels, routed(): pl.pallas_call(functools.partial(routed_kernel, E, host, served, phases,...  54.8 us
    reduce_sum x1, other arithmetic, per_device(): which = jnp.sum(jnp.where(old != old[0], weight, 0)) - 1  1.97 us
    unnamed x1, local copies, waits for them, and re-layouts  1.67 us

profile of v1, /device:TPU:0, one launch (start us, length us, event | category | flops | bytes accessed | tf_op | source)
XLA Modules:
  0.0 60.5 jit_solution(6466982689536959094)
XLA Ops:
  0.0 1.2 %slice.9 = s32[1,1]{1,0:T(1,128)} slice(s32[2,4]{1,0:T(2,128)} %param.19), slice={[0:1], [0:1]} | slice | bytes 8 | tf_op jit(solution)/shard_map/slice | solution.py:623
  1.2 2.0 %fusion = s32[]{:T(128)} fusion(s32[1,4]{1,0:T(1,128)} %constant.11, s32[2,4]{1,0:T(2,128)} %param.19, s32[]{:T(128)} %bitcast.21), kind=kLoop, calls=%fused_computation.1 | loop fusion | flops 11 | bytes 40 | tf_op jit(solution)/shard_map/reduce_sum | solution.py:623
  3.7 55.1 %conditional.1 = (bf16[2,64,1024]{2,1,0:T(8,128)(2,1)}) conditional(s32[]{:T(128)} %clamp.3, (bf16[2,64,4096]{2,1,0:T(8,128)(2,1)}, s32[4]{0:T(128)}, s32[2,2,64]{2,1,0:T(2,128)}, f32[2,2,64]{2,1,0:T(2,128)}, s32[2,2,64]{2,1,0:T(2,128)}, /*index=5*/s32[2,4]{1,0:T(2,128)}, ...), branch_computations={%region_1.2_spmd, %region_2.3_spmd, %region_3.4_spmd, %region_4.5_... | conditional | bytes 8 | solution.py:624
  3.7 54.8 %branch_0_fun.1 = bf16[128,1024]{1,0:T(8,128)(2,1)} custom-call(bf16[128,4096]{1,0:T(8,128)(2,1)} %bitcast.25, s32[2,2,64]{2,1,0:T(2,128)} %get-tuple-element.127.ids, f32[2,2,64]{2,1,0:T(2,128)} %get-tuple-element.128.gates, s32[2,2,64]{2,1,0:T(2,128)} %get-tuple-element.129.replica, s32[2,4]{1,0:T(2,128)} %get-tuple-element.130.table.placement, ...), custom_call_target="tpu_custom_call" | custom-call | tf_op jit(solution)/shard_map/cond/branch_0_fun/pallas_call | solution.py:575
  58.8 1.7 %copy.45 = bf16[2,64,1024]{2,1,0:T(8,128)(2,1)} copy(bf16[2,64,1024]{2,1,0:T(8,128)(2,1)} %get-tuple-element.175) | data formatting | bytes 524288
